TPU v7x, 32 devices: a whole 2x2x4 slice. The times are simulated.
32 devices in a mesh: tm: 8 (over y, x, core), space: 4 (over z).
Axes of the slice: x: 2, y: 2, z: 4, core: 2. Of those that a mesh axis runs over, the one named last changes fastest.
Arguments:
- start_block: float32 [16, 32, 8192], P('tm', None, 'space'), as said below
- stiffness_tiles: float32 [16, 320, 128, 128], P('tm', 'space'), as said below
- tile_columns: int32 [16, 320], P('tm', 'space'), may hold values from 0 to 63, as said below
Outputs:
- ritz_basis: float32 [16, 32, 8192], P('tm', None, 'space')
- first_basis: float32 [16, 32, 8192], P('tm', None, 'space')
- ritz_matrix: float32 [32, 32], replicated
Inputs may be any that keep to these rules, and one draw needn't show every extreme that they name: `tile_columns`: in every slice, block row r has its 5 tiles listed together in row order; the first names column block r, the others distinct column blocks (r + o) mod 64 with 0 < |o| <= 8; in every slice some block row has o = -8 and o = 8. `stiffness_tiles`: real entries. `start_block`: real entries.
All inputs are finite; a program needn't handle non-finite values.
Results may differ from a plain program's by a relative error of at most 0.00018.
Values sent between devices are 32-bit elements; how exact they have to be, the bound alone decides.
No kernel may reach another device: no remote copies, remote signals or barrier semaphores. Data moves between devices by JAX's collectives and lax.ppermute only.
A program may use at most 192 MiB of HBM per device.

v0:
```python
import jax
import jax.numpy as jnp
from jax import lax
from jax.sharding import PartitionSpec as P

TILE = 128
TPR = 5
HB = 8
CENTER = 6.5
RADIUS = 3.5
INFLATION_FACTOR = 0.8
accurate = lax.Precision.HIGHEST


def with_halo(cells, sides, width, closed):
    for axis, dim in sides:
        count = lax.axis_size(axis)
        ends = count if closed else count - 1
        head = lax.slice_in_dim(cells, 0, width, axis=dim)
        tail = lax.slice_in_dim(cells, cells.shape[dim] - width, cells.shape[dim], axis=dim)
        cells = jnp.concatenate(
            [
                lax.ppermute(tail, axis, [(i, (i + 1) % count) for i in range(ends)]),
                cells,
                lax.ppermute(head, axis, [((i + 1) % count, i) for i in range(ends)]),
            ],
            axis=dim,
        )
    return cells


def spatial_component(wide_vectors, tile_groups, column_groups):
    slices, width, extended_points = wide_vectors.shape
    wide_blocks = extended_points // TILE
    out_blocks = tile_groups.shape[1] // TPR

    def one_slice(slice_vec, tile_set, col_list):
        picked = jnp.take(slice_vec.reshape(width, wide_blocks, TILE), col_list, axis=1)
        products = jnp.einsum("nrc,knc->knr", tile_set, picked, precision=accurate)
        return (
            products.reshape(width, out_blocks, TPR, TILE)
            .sum(axis=2)
            .reshape(width, out_blocks * TILE)
        )

    return jax.vmap(one_slice)(wide_vectors, tile_groups, column_groups)


def temporal_component(vectors, degree):
    near_slices = with_halo(vectors, (("tm", 0),), 1, False)
    return degree[:, None, None] * vectors - near_slices[:-2] - near_slices[2:]


def apply_operator(vectors, tile_groups, column_groups, degree):
    extended_points = with_halo(vectors, (("space", 2),), HB * TILE, True)
    return spatial_component(
        extended_points, tile_groups, column_groups
    ) + INFLATION_FACTOR * temporal_component(vectors, degree)


def chebyshev_filter(vectors, operator):
    previous = vectors
    current = (operator(vectors) - CENTER * vectors) / RADIUS
    for step in range(2):
        following = 2.0 * (operator(current) - CENTER * current) / RADIUS - previous
        previous, current = (current, following)
    return current


def gram_terms(left_block, right_block):
    return jnp.einsum("sjp,skp->jk", left_block, right_block, precision=accurate)


def inverse_factor(gram_matrix):
    cholesky_factor = jnp.linalg.cholesky(gram_matrix)
    identity = jnp.eye(gram_matrix.shape[0], dtype=jnp.float32)
    return lax.linalg.triangular_solve(cholesky_factor, identity, left_side=True, lower=True)


def mix_vectors(matrix, vectors):
    return jnp.einsum("jk,skp->sjp", matrix, vectors, precision=accurate)


def body(start_block, stiffness_tiles, tile_columns):
    slices = start_block.shape[0]
    local_points = start_block.shape[2]
    local_blocks = local_points // TILE
    first_block = lax.axis_index("space") * local_blocks
    blocks_all = lax.axis_size("space") * local_blocks
    column_groups = (tile_columns - first_block + HB) % blocks_all
    count_all = slices * local_points * lax.axis_size("tm") * lax.axis_size("space")
    slice_index = lax.axis_index("tm") * slices + jnp.arange(slices, dtype=jnp.int32)
    last_slice = lax.axis_size("tm") * slices - 1
    degree = (
        2.0
        - (slice_index == 0).astype(jnp.float32)
        - (slice_index == last_slice).astype(jnp.float32)
    )

    def operator(vectors):
        return apply_operator(vectors, stiffness_tiles, column_groups, degree)

    def run_filter(vectors):
        return chebyshev_filter(vectors, operator)

    filtered = run_filter(start_block)
    first_gram = lax.psum(gram_terms(filtered, filtered), ("tm", "space")) / count_all
    first_basis = mix_vectors(inverse_factor(first_gram), filtered)
    second = run_filter(first_basis)
    second_gram = lax.psum(gram_terms(second, second), ("tm", "space")) / count_all
    ritz_basis = mix_vectors(inverse_factor(second_gram), second)
    image_block = operator(ritz_basis)
    ritz_matrix = lax.psum(gram_terms(ritz_basis, image_block), ("tm", "space")) / count_all
    return (ritz_basis, first_basis, ritz_matrix)


def solution(mesh):
    placed = (P("tm", None, "space"), P("tm", "space", None, None), P("tm", "space"))
    return jax.shard_map(
        body,
        mesh=mesh,
        in_specs=placed,
        out_specs=(P("tm", None, "space"), P("tm", None, "space"), P()),
        check_vma=False,
    )
```

profile of v0, /device:TPU:0, one launch (start us, length us, event | category | flops | bytes accessed | tf_op | source)
XLA Modules:
  0.0 426.7 jit_solution(2295299034075395820)
XLA Ops:
  14.0 4.2 collective-permute-done.1
  19.3 3.8 gather_fusion
  23.1 19.4 %fusion.12 = f32[2,80,32,128]{3,2,1,0:T(8,128)S(1)} fusion(f32[2,80,128,128]{3,2,1,0:T(8,128)} %param.9, f32[2,80,32,128]{3,2,1,0:T(8,128)} %bitcast.210, pred[2,80]{1,0:T(4,128)(4,1)S(1)} %get-tuple-element.22), kind=kOutput, calls=%fused_computation.19 | convolution fusion | flops 1007288320 | bytes 15728800 | tf_op jit(solution)/shard_map/vmap(nrc,knc->knr)/dot_general | solution.py:39
  52.2 4.1 collective-permute-done.4
  56.3 3.6 collective-permute-done.5
  60.1 3.8 gather_fusion.1
  63.9 20.5 %fusion.10 = f32[2,80,32,128]{3,2,1,0:T(8,128)} fusion(f32[2,80,128,128]{3,2,1,0:T(8,128)} %param.9, f32[2,80,32,128]{3,2,1,0:T(8,128)} %bitcast.211, pred[2,80]{1,0:T(4,128)(4,1)S(1)} %get-tuple-element.22), kind=kOutput, calls=%fused_computation.17 | convolution fusion | flops 1007288320 | bytes 15728800 | tf_op jit(solution)/shard_map/vmap(nrc,knc->knr)/dot_general | solution.py:39
  94.4 4.4 %collective-permute-done.8 = f32[2,32,1024]{2,1,0:T(8,128)S(1)} collective-permute-done((f32[2,32,1024]{2,1,0:T(8,128)S(1)}, f32[2,32,1024]{2,1,0:T(8,128)S(1)}, u32[]{:S(2)}, u32[]{:S(2)}) %collective-permute-start.8) | collective-permute-done | bytes 262176 | tf_op jit(solution)/shard_map/ppermute | solution.py:23
  101.4 3.8 gather_fusion.2
  105.2 20.5 %fusion.8 = f32[2,80,32,128]{3,2,1,0:T(8,128)} fusion(f32[2,80,128,128]{3,2,1,0:T(8,128)} %param.9, f32[2,80,32,128]{3,2,1,0:T(8,128)} %bitcast.212, pred[2,80]{1,0:T(4,128)(4,1)S(1)} %get-tuple-element.22), kind=kOutput, calls=%fused_computation.15 | convolution fusion | flops 1007288320 | bytes 15728800 | tf_op jit(solution)/shard_map/vmap(nrc,knc->knr)/dot_general | solution.py:39
  128.6 40.3 %psum.21 = f32[32,32]{0,1:T(8,128)S(1)} all-reduce(f32[32,32]{0,1:T(8,128)S(1)} %convolution_bitcast_fusion.6), channel_id=1, replica_groups=mesh['tm'=8,'space'=4] {'tm','space'}, use_global_device_ids=true, to_apply=%region_3.5 | all-reduce | flops 1024 | bytes 8192 | tf_op jit(solution)/shard_map/psum | solution.py:107
  189.9 3.8 gather_fusion.3
  193.6 19.4 %fusion.6 = f32[2,80,32,128]{3,2,1,0:T(8,128)S(1)} fusion(f32[2,80,128,128]{3,2,1,0:T(8,128)} %param.9, f32[2,80,32,128]{3,2,1,0:T(8,128)} %bitcast.213, pred[2,80]{1,0:T(4,128)(4,1)S(1)} %get-tuple-element.22), kind=kOutput, calls=%fused_computation.13 | convolution fusion | flops 1007288320 | bytes 15728800 | tf_op jit(solution)/shard_map/vmap(nrc,knc->knr)/dot_general | solution.py:39
  222.7 4.2 collective-permute-done.16
  229.6 3.8 gather_fusion.4
  233.3 20.5 %fusion.4 = f32[2,80,32,128]{3,2,1,0:T(8,128)} fusion(f32[2,80,128,128]{3,2,1,0:T(8,128)} %param.9, f32[2,80,32,128]{3,2,1,0:T(8,128)} %bitcast.214, pred[2,80]{1,0:T(4,128)(4,1)S(1)} %get-tuple-element.22), kind=kOutput, calls=%fused_computation.11 | convolution fusion | flops 1007288320 | bytes 15728800 | tf_op jit(solution)/shard_map/vmap(nrc,knc->knr)/dot_general | solution.py:39
  263.9 4.4 %collective-permute-done.20 = f32[2,32,1024]{2,1,0:T(8,128)S(1)} collective-permute-done((f32[2,32,1024]{2,1,0:T(8,128)S(1)}, f32[2,32,1024]{2,1,0:T(8,128)S(1)}, u32[]{:S(2)}, u32[]{:S(2)}) %collective-permute-start.20) | collective-permute-done | bytes 262176 | tf_op jit(solution)/shard_map/ppermute | solution.py:23
  271.7 3.8 gather_fusion.5
  275.4 20.5 %fusion.2 = f32[2,80,32,128]{3,2,1,0:T(8,128)} fusion(f32[2,80,128,128]{3,2,1,0:T(8,128)} %param.9, f32[2,80,32,128]{3,2,1,0:T(8,128)} %bitcast.215, pred[2,80]{1,0:T(4,128)(4,1)S(1)} %get-tuple-element.22), kind=kOutput, calls=%fused_computation.9 | convolution fusion | flops 1007288320 | bytes 15728800 | tf_op jit(solution)/shard_map/vmap(nrc,knc->knr)/dot_general | solution.py:39
  298.8 39.3 %psum.22 = f32[32,32]{0,1:T(8,128)S(1)} all-reduce(f32[32,32]{0,1:T(8,128)S(1)} %convolution_bitcast_fusion.4), channel_id=1, replica_groups=mesh['tm'=8,'space'=4] {'tm','space'}, use_global_device_ids=true, to_apply=%region_9.13 | all-reduce | flops 1024 | bytes 8192 | tf_op jit(solution)/shard_map/psum | solution.py:110
  353.3 3.6 collective-permute-done.24
  359.8 3.8 gather_fusion.6
  363.6 19.4 %fusion = f32[2,80,32,128]{3,2,1,0:T(8,128)S(1)} fusion(f32[2,80,128,128]{3,2,1,0:T(8,128)} %param.9, f32[2,80,32,128]{3,2,1,0:T(8,128)} %bitcast.209, pred[2,80]{1,0:T(4,128)(4,1)S(1)} %get-tuple-element.22), kind=kOutput, calls=%fused_computation.7 | convolution fusion | flops 1007288320 | bytes 15728800 | tf_op jit(solution)/shard_map/vmap(nrc,knc->knr)/dot_general | solution.py:39
  386.0 39.8 %psum.23 = f32[32,32]{0,1:T(8,128)S(1)} all-reduce(f32[32,32]{0,1:T(8,128)S(1)} %convolution_bitcast_fusion.2), channel_id=1, replica_groups=mesh['tm'=8,'space'=4] {'tm','space'}, use_global_device_ids=true, to_apply=%region_11.15 | all-reduce | flops 1024 | bytes 8192 | tf_op jit(solution)/shard_map/psum | solution.py:113
  (119 shorter events, 111.1 us)
Async XLA Ops:
  1.7 12.3 %collective-permute-start = (f32[2,32,1024]{2,1,0:T(8,128)S(1)}, f32[2,32,1024]{2,1,0:T(8,128)S(1)}, u32[]{:S(2)}, u32[]{:S(2)}) collective-permute-start(f32[2,32,1024]{2,1,0:T(8,128)S(1)} %get-tuple-element.48), channel_id=1, source_target_pairs={{0,1},{1,2},{2,3},{3,0},{4,5},{5,6},{6,7},{7,4},{8,9},{9,10},{10,1... | collective-permute-start | bytes 786440 | tf_op jit(solution)/shard_map/ppermute | solution.py:23
  4.8 13.4 %collective-permute-start.1 = (f32[2,32,1024]{2,1,0:T(8,128)S(1)}, f32[2,32,1024]{2,1,0:T(8,128)S(1)}, u32[]{:S(2)}, u32[]{:S(2)}) collective-permute-start(f32[2,32,1024]{2,1,0:T(8,128)S(1)} %get-tuple-element.49), channel_id=1, source_target_pairs={{1,0},{2,1},{3,2},{0,3},{5,4},{6,5},{7,6},{4,7},{9,8},{10,9},{11,1... | collective-permute-start | bytes 786440 | tf_op jit(solution)/shard_map/ppermute | solution.py:25
  8.6 35.1 %collective-permute-start.2 = (f32[1,32,2048]{2,1,0:T(8,128)}, f32[1,32,2048]{2,1,0:T(8,128)}, u32[]{:S(2)}, u32[]{:S(2)}) collective-permute-start(f32[1,32,2048]{2,1,0:T(8,128)} %get-tuple-element.50), channel_id=1, source_target_pairs={{0,4},{4,8},{8,12},{12,16},{16,20},{20,24},{24,28},{1,5},{5,9},{9,... | collective-permute-start | bytes 786440 | tf_op jit(solution)/shard_map/ppermute | solution.py:23
  10.8 32.9 %collective-permute-start.3 = (f32[1,32,2048]{2,1,0:T(8,128)S(1)}, f32[1,32,2048]{2,1,0:T(8,128)}, u32[]{:S(2)}, u32[]{:S(2)}) collective-permute-start(f32[1,32,2048]{2,1,0:T(8,128)S(1)} %get-tuple-element.51), channel_id=1, source_target_pairs={{4,0},{8,4},{12,8},{16,12},{20,16},{24,20},{28,24},{5,1},{9,5},{13... | collective-permute-start | bytes 786440 | tf_op jit(solution)/shard_map/ppermute | solution.py:25
  45.2 11.1 %collective-permute-start.4 = (f32[2,32,1024]{2,1,0:T(8,128)S(1)}, f32[2,32,1024]{2,1,0:T(8,128)S(1)}, u32[]{:S(2)}, u32[]{:S(2)}) collective-permute-start(f32[2,32,1024]{2,1,0:T(8,128)S(1)} %get-tuple-element.46), channel_id=1, source_target_pairs={{0,1},{1,2},{2,3},{3,0},{4,5},{5,6},{6,7},{7,4},{8,9},{9,10},{10,1... | collective-permute-start | bytes 786440 | tf_op jit(solution)/shard_map/ppermute | solution.py:23
  46.4 13.6 %collective-permute-start.5 = (f32[2,32,1024]{2,1,0:T(8,128)S(1)}, f32[2,32,1024]{2,1,0:T(8,128)S(1)}, u32[]{:S(2)}, u32[]{:S(2)}) collective-permute-start(f32[2,32,1024]{2,1,0:T(8,128)S(1)} %get-tuple-element.47), channel_id=1, source_target_pairs={{1,0},{2,1},{3,2},{0,3},{5,4},{6,5},{7,6},{4,7},{9,8},{10,9},{11,1... | collective-permute-start | bytes 786440 | tf_op jit(solution)/shard_map/ppermute | solution.py:25
  49.1 37.3 %collective-permute-start.6 = (f32[1,32,2048]{2,1,0:T(8,128)S(1)}, f32[1,32,2048]{2,1,0:T(8,128)S(1)}, u32[]{:S(2)}, u32[]{:S(2)}) collective-permute-start(f32[1,32,2048]{2,1,0:T(8,128)S(1)} %get-tuple-element.44), channel_id=1, source_target_pairs={{0,4},{4,8},{8,12},{12,16},{16,20},{20,24},{24,28},{1,5},{5,9},{9,... | collective-permute-start | bytes 786440 | tf_op jit(solution)/shard_map/ppermute | solution.py:23
  50.4 36.0 %collective-permute-start.7 = (f32[1,32,2048]{2,1,0:T(8,128)S(1)}, f32[1,32,2048]{2,1,0:T(8,128)}, u32[]{:S(2)}, u32[]{:S(2)}) collective-permute-start(f32[1,32,2048]{2,1,0:T(8,128)S(1)} %get-tuple-element.45), channel_id=1, source_target_pairs={{4,0},{8,4},{12,8},{16,12},{20,16},{24,20},{28,24},{5,1},{9,5},{13... | collective-permute-start | bytes 786440 | tf_op jit(solution)/shard_map/ppermute | solution.py:25
  88.1 13.1 %collective-permute-start.9 = (f32[2,32,1024]{2,1,0:T(8,128)S(1)}, f32[2,32,1024]{2,1,0:T(8,128)S(1)}, u32[]{:S(2)}, u32[]{:S(2)}) collective-permute-start(f32[2,32,1024]{2,1,0:T(8,128)S(1)} %get-tuple-element.43), channel_id=1, source_target_pairs={{1,0},{2,1},{3,2},{0,3},{5,4},{6,5},{7,6},{4,7},{9,8},{10,9},{11,1... | collective-permute-start | bytes 786440 | tf_op jit(solution)/shard_map/ppermute | solution.py:25
  91.6 36.1 %collective-permute-start.10 = (f32[1,32,2048]{2,1,0:T(8,128)S(1)}, f32[1,32,2048]{2,1,0:T(8,128)S(1)}, u32[]{:S(2)}, u32[]{:S(2)}) collective-permute-start(f32[1,32,2048]{2,1,0:T(8,128)S(1)} %get-tuple-element.40), channel_id=1, source_target_pairs={{0,4},{4,8},{8,12},{12,16},{16,20},{20,24},{24,28},{1,5},{5,9},{9,... | collective-permute-start | bytes 786440 | tf_op jit(solution)/shard_map/ppermute | solution.py:23
  93.0 34.8 %collective-permute-start.11 = (f32[1,32,2048]{2,1,0:T(8,128)S(1)}, f32[1,32,2048]{2,1,0:T(8,128)S(1)}, u32[]{:S(2)}, u32[]{:S(2)}) collective-permute-start(f32[1,32,2048]{2,1,0:T(8,128)S(1)} %get-tuple-element.41), channel_id=1, source_target_pairs={{4,0},{8,4},{12,8},{16,12},{20,16},{24,20},{28,24},{5,1},{9,5},{13... | collective-permute-start | bytes 786440 | tf_op jit(solution)/shard_map/ppermute | solution.py:25
  177.1 12.6 %collective-permute-start.13 = (f32[2,32,1024]{2,1,0:T(8,128)S(1)}, f32[2,32,1024]{2,1,0:T(8,128)S(1)}, u32[]{:S(2)}, u32[]{:S(2)}) collective-permute-start(f32[2,32,1024]{2,1,0:T(8,128)S(1)} %get-tuple-element.37), channel_id=1, source_target_pairs={{1,0},{2,1},{3,2},{0,3},{5,4},{6,5},{7,6},{4,7},{9,8},{10,9},{11,1... | collective-permute-start | bytes 786440 | tf_op jit(solution)/shard_map/ppermute | solution.py:25
  181.2 33.0 %collective-permute-start.14 = (f32[1,32,2048]{2,1,0:T(8,128)}, f32[1,32,2048]{2,1,0:T(8,128)}, u32[]{:S(2)}, u32[]{:S(2)}) collective-permute-start(f32[1,32,2048]{2,1,0:T(8,128)} %get-tuple-element.38), channel_id=1, source_target_pairs={{0,4},{4,8},{8,12},{12,16},{16,20},{20,24},{24,28},{1,5},{5,9},{9,... | collective-permute-start | bytes 786440 | tf_op jit(solution)/shard_map/ppermute | solution.py:23
  183.2 31.0 %collective-permute-start.15 = (f32[1,32,2048]{2,1,0:T(8,128)S(1)}, f32[1,32,2048]{2,1,0:T(8,128)}, u32[]{:S(2)}, u32[]{:S(2)}) collective-permute-start(f32[1,32,2048]{2,1,0:T(8,128)S(1)} %get-tuple-element.39), channel_id=1, source_target_pairs={{4,0},{8,4},{12,8},{16,12},{20,16},{24,20},{28,24},{5,1},{9,5},{13... | collective-permute-start | bytes 786440 | tf_op jit(solution)/shard_map/ppermute | solution.py:25
  216.9 12.5 %collective-permute-start.17 = (f32[2,32,1024]{2,1,0:T(8,128)S(1)}, f32[2,32,1024]{2,1,0:T(8,128)S(1)}, u32[]{:S(2)}, u32[]{:S(2)}) collective-permute-start(f32[2,32,1024]{2,1,0:T(8,128)S(1)} %get-tuple-element.35), channel_id=1, source_target_pairs={{1,0},{2,1},{3,2},{0,3},{5,4},{6,5},{7,6},{4,7},{9,8},{10,9},{11,1... | collective-permute-start | bytes 786440 | tf_op jit(solution)/shard_map/ppermute | solution.py:25
  219.6 36.3 %collective-permute-start.18 = (f32[1,32,2048]{2,1,0:T(8,128)S(1)}, f32[1,32,2048]{2,1,0:T(8,128)S(1)}, u32[]{:S(2)}, u32[]{:S(2)}) collective-permute-start(f32[1,32,2048]{2,1,0:T(8,128)S(1)} %get-tuple-element.32), channel_id=1, source_target_pairs={{0,4},{4,8},{8,12},{12,16},{16,20},{20,24},{24,28},{1,5},{5,9},{9,... | collective-permute-start | bytes 786440 | tf_op jit(solution)/shard_map/ppermute | solution.py:23
  220.9 35.0 %collective-permute-start.19 = (f32[1,32,2048]{2,1,0:T(8,128)S(1)}, f32[1,32,2048]{2,1,0:T(8,128)}, u32[]{:S(2)}, u32[]{:S(2)}) collective-permute-start(f32[1,32,2048]{2,1,0:T(8,128)S(1)} %get-tuple-element.33), channel_id=1, source_target_pairs={{4,0},{8,4},{12,8},{16,12},{20,16},{24,20},{28,24},{5,1},{9,5},{13... | collective-permute-start | bytes 786440 | tf_op jit(solution)/shard_map/ppermute | solution.py:25
  258.0 13.5 %collective-permute-start.21 = (f32[2,32,1024]{2,1,0:T(8,128)S(1)}, f32[2,32,1024]{2,1,0:T(8,128)S(1)}, u32[]{:S(2)}, u32[]{:S(2)}) collective-permute-start(f32[2,32,1024]{2,1,0:T(8,128)S(1)} %get-tuple-element.31), channel_id=1, source_target_pairs={{1,0},{2,1},{3,2},{0,3},{5,4},{6,5},{7,6},{4,7},{9,8},{10,9},{11,1... | collective-permute-start | bytes 786440 | tf_op jit(solution)/shard_map/ppermute | solution.py:25
  261.1 36.9 %collective-permute-start.22 = (f32[1,32,2048]{2,1,0:T(8,128)S(1)}, f32[1,32,2048]{2,1,0:T(8,128)S(1)}, u32[]{:S(2)}, u32[]{:S(2)}) collective-permute-start(f32[1,32,2048]{2,1,0:T(8,128)S(1)} %get-tuple-element.28), channel_id=1, source_target_pairs={{0,4},{4,8},{8,12},{12,16},{16,20},{20,24},{24,28},{1,5},{5,9},{9,... | collective-permute-start | bytes 786440 | tf_op jit(solution)/shard_map/ppermute | solution.py:23
  262.4 35.6 %collective-permute-start.23 = (f32[1,32,2048]{2,1,0:T(8,128)S(1)}, f32[1,32,2048]{2,1,0:T(8,128)S(1)}, u32[]{:S(2)}, u32[]{:S(2)}) collective-permute-start(f32[1,32,2048]{2,1,0:T(8,128)S(1)} %get-tuple-element.29), channel_id=1, source_target_pairs={{4,0},{8,4},{12,8},{16,12},{20,16},{24,20},{28,24},{5,1},{9,5},{13... | collective-permute-start | bytes 786440 | tf_op jit(solution)/shard_map/ppermute | solution.py:25
  345.8 11.1 %collective-permute-start.24 = (f32[2,32,1024]{2,1,0:T(8,128)S(1)}, f32[2,32,1024]{2,1,0:T(8,128)S(1)}, u32[]{:S(2)}, u32[]{:S(2)}) collective-permute-start(f32[2,32,1024]{2,1,0:T(8,128)S(1)} %get-tuple-element.26), channel_id=1, source_target_pairs={{0,1},{1,2},{2,3},{3,0},{4,5},{5,6},{6,7},{7,4},{8,9},{9,10},{10,1... | collective-permute-start | bytes 786440 | tf_op jit(solution)/shard_map/ppermute | solution.py:23
  347.1 12.6 %collective-permute-start.25 = (f32[2,32,1024]{2,1,0:T(8,128)S(1)}, f32[2,32,1024]{2,1,0:T(8,128)S(1)}, u32[]{:S(2)}, u32[]{:S(2)}) collective-permute-start(f32[2,32,1024]{2,1,0:T(8,128)S(1)} %get-tuple-element.27), channel_id=1, source_target_pairs={{1,0},{2,1},{3,2},{0,3},{5,4},{6,5},{7,6},{4,7},{9,8},{10,9},{11,1... | collective-permute-start | bytes 786440 | tf_op jit(solution)/shard_map/ppermute | solution.py:25
  350.5 33.7 %collective-permute-start.26 = (f32[1,32,2048]{2,1,0:T(8,128)}, f32[1,32,2048]{2,1,0:T(8,128)S(1)}, u32[]{:S(2)}, u32[]{:S(2)}) collective-permute-start(f32[1,32,2048]{2,1,0:T(8,128)} %get-tuple-element.24), channel_id=1, source_target_pairs={{0,4},{4,8},{8,12},{12,16},{16,20},{20,24},{24,28},{1,5},{5,9},{9,... | collective-permute-start | bytes 786440 | tf_op jit(solution)/shard_map/ppermute | solution.py:23
  351.8 32.4 %collective-permute-start.27 = (f32[1,32,2048]{2,1,0:T(8,128)}, f32[1,32,2048]{2,1,0:T(8,128)}, u32[]{:S(2)}, u32[]{:S(2)}) collective-permute-start(f32[1,32,2048]{2,1,0:T(8,128)} %get-tuple-element.25), channel_id=1, source_target_pairs={{4,0},{8,4},{12,8},{16,12},{20,16},{24,20},{28,24},{5,1},{9,5},{13... | collective-permute-start | bytes 786440 | tf_op jit(solution)/shard_map/ppermute | solution.py:25
  (7 other events, 163.4 us)
where the time goes:
time: 435 us; the launch traced here: 427 us
  matrix products  145 us (33%)
  blocking collectives  119 us (27%)
  starting transfers between devices  49.8 us (11%)
  waiting for transfers between devices  45.7 us (11%)
  other arithmetic  33.7 us (8%)
  local copies, waits for them, and re-layouts  32.1 us (7%)
    dot_general x7, matrix products, one_slice(): products = jnp.einsum('nrc,knc->knr', tile_set, picked, precision=accurate)  140 us
    psum x1, blocking collectives, body(): lax.psum(gram_terms(filtered, filtered), ('tm', 'space')) / count_all  40.3 us
    psum x1, blocking collectives, body(): lax.psum(gram_terms(ritz_basis, image_block), ('tm', 'space')) / count_all  39.8 us
    psum x1, blocking collectives, body(): lax.psum(gram_terms(second, second), ('tm', 'space')) / count_all  39.3 us
    ppermute x14, starting transfers between devices, with_halo(): lax.ppermute(head, axis, [((i + 1) % count, i) for i in range(ends)])  30.5 us
    gather x8, local copies, waits for them, and re-layouts, one_slice(): jnp.take(slice_vec.reshape(width, wide_blocks, TILE), col_list, axis=1)  26.4 us
    ppermute x14, waiting for transfers between devices, with_halo(): lax.ppermute(tail, axis, [(i, (i + 1) % count) for i in range(ends)])  24.7 us
    ppermute x14, waiting for transfers between devices, with_halo(): lax.ppermute(head, axis, [((i + 1) % count, i) for i in range(ends)])  21.1 us
  transfers between devices with their start and end apart: 28, of which 14 were waited for; matrix products, arithmetic and copies ran while one was open for 43% of the time, Pallas kernels for 0%

commit v1 on v0

--- a/solution.py
+++ b/solution.py
@@ -10,6 +10,7 @@
 RADIUS = 3.5
 INFLATION_FACTOR = 0.8
 accurate = lax.Precision.HIGHEST
+change_kinds = lambda row_data, net_axis: jnp.sum(lax.all_gather(row_data, axis_name=net_axis), 0)
 
 
 def with_halo(cells, sides, width, closed):
@@ -104,7 +105,7 @@
         return chebyshev_filter(vectors, operator)
 
     filtered = run_filter(start_block)
-    first_gram = lax.psum(gram_terms(filtered, filtered), ("tm", "space")) / count_all
+    first_gram = change_kinds(gram_terms(filtered, filtered), ("tm", "space")) / count_all
     first_basis = mix_vectors(inverse_factor(first_gram), filtered)
     second = run_filter(first_basis)
     second_gram = lax.psum(gram_terms(second, second), ("tm", "space")) / count_all

time: 435 us -> 460 us (1.057)
  blocking collectives: 119 us -> 149 us
    all_gather x0 -> x1, blocking collectives: none -> 69.6 us  [lax.all_gather(row_data, axis_name=net_axis)]
    psum x1 -> x0, blocking collectives: 40.3 us -> none  [body(): lax.psum(gram_terms(filtered, filtered), ('tm', 'space')) / count_all]
  transfers between devices with their start and end apart: 28 -> 28, of which waited for: 14 -> 14; matrix products, arithmetic and copies ran while one was open for 43% -> 41% of each run, Pallas kernels for 0% -> 0%
where the time goes in v1:
time: 460 us; the launch traced here: 452 us
  blocking collectives  149 us (32%)
  matrix products  145 us (32%)
  starting transfers between devices  49.8 us (11%)
  waiting for transfers between devices  41.5 us (9%)
  other arithmetic  33.8 us (7%)
  local copies, waits for them, and re-layouts  32.1 us (7%)
    dot_general x7, matrix products, one_slice(): products = jnp.einsum('nrc,knc->knr', tile_set, picked, precision=accurate)  140 us
    all_gather x1, blocking collectives, lax.all_gather(row_data, axis_name=net_axis)  69.6 us
    psum x1, blocking collectives, body(): lax.psum(gram_terms(ritz_basis, image_block), ('tm', 'space')) / count_all  39.8 us
    psum x1, blocking collectives, body(): lax.psum(gram_terms(second, second), ('tm', 'space')) / count_all  39.4 us
    ppermute x14, starting transfers between devices, with_halo(): lax.ppermute(head, axis, [((i + 1) % count, i) for i in range(ends)])  32.8 us
    gather x8, local copies, waits for them, and re-layouts, one_slice(): jnp.take(slice_vec.reshape(width, wide_blocks, TILE), col_list, axis=1)  26.4 us
    ppermute x14, waiting for transfers between devices, with_halo(): lax.ppermute(tail, axis, [(i, (i + 1) % count) for i in range(ends)])  22 us
    ppermute x14, waiting for transfers between devices, with_halo(): lax.ppermute(head, axis, [((i + 1) % count, i) for i in range(ends)])  19.5 us
  transfers between devices with their start and end apart: 28, of which 14 were waited for; matrix products, arithmetic and copies ran while one was open for 41% of the time, Pallas kernels for 0%

profile of v1, /device:TPU:0, one launch (start us, length us, event | category | flops | bytes accessed | tf_op | source)
XLA Modules:
  0.0 452.1 jit_solution(8298048411117884415)
XLA Ops:
  14.0 4.2 collective-permute-done.1
  19.3 3.8 gather_fusion
  23.1 19.4 %fusion.12 = f32[2,80,32,128]{3,2,1,0:T(8,128)S(1)} fusion(f32[2,80,128,128]{3,2,1,0:T(8,128)} %param.9, f32[2,80,32,128]{3,2,1,0:T(8,128)} %bitcast.211, pred[2,80]{1,0:T(4,128)(4,1)S(1)} %get-tuple-element.22), kind=kOutput, calls=%fused_computation.19 | convolution fusion | flops 1007288320 | bytes 15728800 | tf_op jit(solution)/shard_map/vmap(nrc,knc->knr)/dot_general | solution.py:40
  52.2 4.1 collective-permute-done.4
  60.1 3.8 gather_fusion.1
  63.9 20.5 %fusion.10 = f32[2,80,32,128]{3,2,1,0:T(8,128)} fusion(f32[2,80,128,128]{3,2,1,0:T(8,128)} %param.9, f32[2,80,32,128]{3,2,1,0:T(8,128)} %bitcast.212, pred[2,80]{1,0:T(4,128)(4,1)S(1)} %get-tuple-element.22), kind=kOutput, calls=%fused_computation.17 | convolution fusion | flops 1007288320 | bytes 15728800 | tf_op jit(solution)/shard_map/vmap(nrc,knc->knr)/dot_general | solution.py:40
  94.4 4.4 collective-permute-done.8
  101.4 3.8 gather_fusion.2
  105.2 20.5 %fusion.8 = f32[2,80,32,128]{3,2,1,0:T(8,128)} fusion(f32[2,80,128,128]{3,2,1,0:T(8,128)} %param.9, f32[2,80,32,128]{3,2,1,0:T(8,128)} %bitcast.213, pred[2,80]{1,0:T(4,128)(4,1)S(1)} %get-tuple-element.22), kind=kOutput, calls=%fused_computation.15 | convolution fusion | flops 1007288320 | bytes 15728800 | tf_op jit(solution)/shard_map/vmap(nrc,knc->knr)/dot_general | solution.py:40
  128.6 69.6 %all-gather = f32[1024,32]{1,0:T(8,128)S(1)} all-gather(f32[32,32]{1,0:T(8,128)S(1)} %convolution_bitcast_fusion.6), channel_id=2, replica_groups=mesh['tm'=8,'space'=4] {'tm','space'}, dimensions={0}, use_global_device_ids=true | all-gather | bytes 135168 | tf_op jit(solution)/shard_map/all_gather | solution.py:13
  215.5 3.8 gather_fusion.3
  219.2 19.4 %fusion.6 = f32[2,80,32,128]{3,2,1,0:T(8,128)S(1)} fusion(f32[2,80,128,128]{3,2,1,0:T(8,128)} %param.9, f32[2,80,32,128]{3,2,1,0:T(8,128)} %bitcast.214, pred[2,80]{1,0:T(4,128)(4,1)S(1)} %get-tuple-element.22), kind=kOutput, calls=%fused_computation.13 | convolution fusion | flops 1007288320 | bytes 15728800 | tf_op jit(solution)/shard_map/vmap(nrc,knc->knr)/dot_general | solution.py:40
  241.4 3.8 collective-permute-start.17
  248.3 4.2 collective-permute-done.16
  255.3 3.8 gather_fusion.4
  259.1 20.5 %fusion.4 = f32[2,80,32,128]{3,2,1,0:T(8,128)} fusion(f32[2,80,128,128]{3,2,1,0:T(8,128)} %param.9, f32[2,80,32,128]{3,2,1,0:T(8,128)} %bitcast.215, pred[2,80]{1,0:T(4,128)(4,1)S(1)} %get-tuple-element.22), kind=kOutput, calls=%fused_computation.11 | convolution fusion | flops 1007288320 | bytes 15728800 | tf_op jit(solution)/shard_map/vmap(nrc,knc->knr)/dot_general | solution.py:40
  283.0 3.8 collective-permute-start.21
  289.6 4.4 collective-permute-done.20
  296.9 3.8 gather_fusion.5
  300.7 20.5 %fusion.2 = f32[2,80,32,128]{3,2,1,0:T(8,128)} fusion(f32[2,80,128,128]{3,2,1,0:T(8,128)} %param.9, f32[2,80,32,128]{3,2,1,0:T(8,128)} %bitcast.216, pred[2,80]{1,0:T(4,128)(4,1)S(1)} %get-tuple-element.22), kind=kOutput, calls=%fused_computation.9 | convolution fusion | flops 1007288320 | bytes 15728800 | tf_op jit(solution)/shard_map/vmap(nrc,knc->knr)/dot_general | solution.py:40
  324.1 39.4 %psum.14 = f32[32,32]{0,1:T(8,128)S(1)} all-reduce(f32[32,32]{0,1:T(8,128)S(1)} %convolution_bitcast_fusion.4), channel_id=1, replica_groups=mesh['tm'=8,'space'=4] {'tm','space'}, use_global_device_ids=true, to_apply=%region_9.13 | all-reduce | flops 1024 | bytes 8192 | tf_op jit(solution)/shard_map/psum | solution.py:111
  385.2 3.8 gather_fusion.6
  388.9 19.4 %fusion = f32[2,80,32,128]{3,2,1,0:T(8,128)S(1)} fusion(f32[2,80,128,128]{3,2,1,0:T(8,128)} %param.9, f32[2,80,32,128]{3,2,1,0:T(8,128)} %bitcast.210, pred[2,80]{1,0:T(4,128)(4,1)S(1)} %get-tuple-element.22), kind=kOutput, calls=%fused_computation.7 | convolution fusion | flops 1007288320 | bytes 15728800 | tf_op jit(solution)/shard_map/vmap(nrc,knc->knr)/dot_general | solution.py:40
  411.3 39.8 %psum.15 = f32[32,32]{0,1:T(8,128)S(1)} all-reduce(f32[32,32]{0,1:T(8,128)S(1)} %convolution_bitcast_fusion.2), channel_id=1, replica_groups=mesh['tm'=8,'space'=4] {'tm','space'}, use_global_device_ids=true, to_apply=%region_11.15 | all-reduce | flops 1024 | bytes 8192 | tf_op jit(solution)/shard_map/psum | solution.py:114
  (121 shorter events, 106.5 us)
Async XLA Ops:
  1.7 12.3 %collective-permute-start = (f32[2,32,1024]{2,1,0:T(8,128)S(1)}, f32[2,32,1024]{2,1,0:T(8,128)S(1)}, u32[]{:S(2)}, u32[]{:S(2)}) collective-permute-start(f32[2,32,1024]{2,1,0:T(8,128)S(1)} %get-tuple-element.48), channel_id=1, source_target_pairs={{0,1},{1,2},{2,3},{3,0},{4,5},{5,6},{6,7},{7,4},{8,9},{9,10},{10,1... | collective-permute-start | bytes 786440 | tf_op jit(solution)/shard_map/ppermute | solution.py:24
  4.8 13.4 %collective-permute-start.1 = (f32[2,32,1024]{2,1,0:T(8,128)S(1)}, f32[2,32,1024]{2,1,0:T(8,128)S(1)}, u32[]{:S(2)}, u32[]{:S(2)}) collective-permute-start(f32[2,32,1024]{2,1,0:T(8,128)S(1)} %get-tuple-element.49), channel_id=1, source_target_pairs={{1,0},{2,1},{3,2},{0,3},{5,4},{6,5},{7,6},{4,7},{9,8},{10,9},{11,1... | collective-permute-start | bytes 786440 | tf_op jit(solution)/shard_map/ppermute | solution.py:26
  8.6 35.1 %collective-permute-start.2 = (f32[1,32,2048]{2,1,0:T(8,128)}, f32[1,32,2048]{2,1,0:T(8,128)}, u32[]{:S(2)}, u32[]{:S(2)}) collective-permute-start(f32[1,32,2048]{2,1,0:T(8,128)} %get-tuple-element.50), channel_id=1, source_target_pairs={{0,4},{4,8},{8,12},{12,16},{16,20},{20,24},{24,28},{1,5},{5,9},{9,... | collective-permute-start | bytes 786440 | tf_op jit(solution)/shard_map/ppermute | solution.py:24
  10.8 32.9 %collective-permute-start.3 = (f32[1,32,2048]{2,1,0:T(8,128)S(1)}, f32[1,32,2048]{2,1,0:T(8,128)}, u32[]{:S(2)}, u32[]{:S(2)}) collective-permute-start(f32[1,32,2048]{2,1,0:T(8,128)S(1)} %get-tuple-element.51), channel_id=1, source_target_pairs={{4,0},{8,4},{12,8},{16,12},{20,16},{24,20},{28,24},{5,1},{9,5},{13... | collective-permute-start | bytes 786440 | tf_op jit(solution)/shard_map/ppermute | solution.py:26
  45.2 11.1 %collective-permute-start.4 = (f32[2,32,1024]{2,1,0:T(8,128)S(1)}, f32[2,32,1024]{2,1,0:T(8,128)S(1)}, u32[]{:S(2)}, u32[]{:S(2)}) collective-permute-start(f32[2,32,1024]{2,1,0:T(8,128)S(1)} %get-tuple-element.46), channel_id=1, source_target_pairs={{0,1},{1,2},{2,3},{3,0},{4,5},{5,6},{6,7},{7,4},{8,9},{9,10},{10,1... | collective-permute-start | bytes 786440 | tf_op jit(solution)/shard_map/ppermute | solution.py:24
  46.4 13.6 %collective-permute-start.5 = (f32[2,32,1024]{2,1,0:T(8,128)S(1)}, f32[2,32,1024]{2,1,0:T(8,128)S(1)}, u32[]{:S(2)}, u32[]{:S(2)}) collective-permute-start(f32[2,32,1024]{2,1,0:T(8,128)S(1)} %get-tuple-element.47), channel_id=1, source_target_pairs={{1,0},{2,1},{3,2},{0,3},{5,4},{6,5},{7,6},{4,7},{9,8},{10,9},{11,1... | collective-permute-start | bytes 786440 | tf_op jit(solution)/shard_map/ppermute | solution.py:26
  49.1 37.3 %collective-permute-start.6 = (f32[1,32,2048]{2,1,0:T(8,128)S(1)}, f32[1,32,2048]{2,1,0:T(8,128)S(1)}, u32[]{:S(2)}, u32[]{:S(2)}) collective-permute-start(f32[1,32,2048]{2,1,0:T(8,128)S(1)} %get-tuple-element.44), channel_id=1, source_target_pairs={{0,4},{4,8},{8,12},{12,16},{16,20},{20,24},{24,28},{1,5},{5,9},{9,... | collective-permute-start | bytes 786440 | tf_op jit(solution)/shard_map/ppermute | solution.py:24
  50.4 36.0 %collective-permute-start.7 = (f32[1,32,2048]{2,1,0:T(8,128)S(1)}, f32[1,32,2048]{2,1,0:T(8,128)}, u32[]{:S(2)}, u32[]{:S(2)}) collective-permute-start(f32[1,32,2048]{2,1,0:T(8,128)S(1)} %get-tuple-element.45), channel_id=1, source_target_pairs={{4,0},{8,4},{12,8},{16,12},{20,16},{24,20},{28,24},{5,1},{9,5},{13... | collective-permute-start | bytes 786440 | tf_op jit(solution)/shard_map/ppermute | solution.py:26
  88.1 13.1 %collective-permute-start.9 = (f32[2,32,1024]{2,1,0:T(8,128)S(1)}, f32[2,32,1024]{2,1,0:T(8,128)S(1)}, u32[]{:S(2)}, u32[]{:S(2)}) collective-permute-start(f32[2,32,1024]{2,1,0:T(8,128)S(1)} %get-tuple-element.43), channel_id=1, source_target_pairs={{1,0},{2,1},{3,2},{0,3},{5,4},{6,5},{7,6},{4,7},{9,8},{10,9},{11,1... | collective-permute-start | bytes 786440 | tf_op jit(solution)/shard_map/ppermute | solution.py:26
  91.6 36.1 %collective-permute-start.10 = (f32[1,32,2048]{2,1,0:T(8,128)S(1)}, f32[1,32,2048]{2,1,0:T(8,128)S(1)}, u32[]{:S(2)}, u32[]{:S(2)}) collective-permute-start(f32[1,32,2048]{2,1,0:T(8,128)S(1)} %get-tuple-element.40), channel_id=1, source_target_pairs={{0,4},{4,8},{8,12},{12,16},{16,20},{20,24},{24,28},{1,5},{5,9},{9,... | collective-permute-start | bytes 786440 | tf_op jit(solution)/shard_map/ppermute | solution.py:24
  93.0 34.8 %collective-permute-start.11 = (f32[1,32,2048]{2,1,0:T(8,128)S(1)}, f32[1,32,2048]{2,1,0:T(8,128)S(1)}, u32[]{:S(2)}, u32[]{:S(2)}) collective-permute-start(f32[1,32,2048]{2,1,0:T(8,128)S(1)} %get-tuple-element.41), channel_id=1, source_target_pairs={{4,0},{8,4},{12,8},{16,12},{20,16},{24,20},{28,24},{5,1},{9,5},{13... | collective-permute-start | bytes 786440 | tf_op jit(solution)/shard_map/ppermute | solution.py:26
  210.6 29.2 %collective-permute-start.14 = (f32[1,32,2048]{2,1,0:T(8,128)}, f32[1,32,2048]{2,1,0:T(8,128)}, u32[]{:S(2)}, u32[]{:S(2)}) collective-permute-start(f32[1,32,2048]{2,1,0:T(8,128)} %get-tuple-element.38), channel_id=1, source_target_pairs={{0,4},{4,8},{8,12},{12,16},{16,20},{20,24},{24,28},{1,5},{5,9},{9,... | collective-permute-start | bytes 786440 | tf_op jit(solution)/shard_map/ppermute | solution.py:24
  212.6 27.2 %collective-permute-start.15 = (f32[1,32,2048]{2,1,0:T(8,128)S(1)}, f32[1,32,2048]{2,1,0:T(8,128)}, u32[]{:S(2)}, u32[]{:S(2)}) collective-permute-start(f32[1,32,2048]{2,1,0:T(8,128)S(1)} %get-tuple-element.39), channel_id=1, source_target_pairs={{4,0},{8,4},{12,8},{16,12},{20,16},{24,20},{28,24},{5,1},{9,5},{13... | collective-permute-start | bytes 786440 | tf_op jit(solution)/shard_map/ppermute | solution.py:26
  241.3 11.1 %collective-permute-start.16 = (f32[2,32,1024]{2,1,0:T(8,128)S(1)}, f32[2,32,1024]{2,1,0:T(8,128)S(1)}, u32[]{:S(2)}, u32[]{:S(2)}) collective-permute-start(f32[2,32,1024]{2,1,0:T(8,128)S(1)} %get-tuple-element.34), channel_id=1, source_target_pairs={{0,1},{1,2},{2,3},{3,0},{4,5},{5,6},{6,7},{7,4},{8,9},{9,10},{10,1... | collective-permute-start | bytes 786440 | tf_op jit(solution)/shard_map/ppermute | solution.py:24
  241.4 13.7 %collective-permute-start.17 = (f32[2,32,1024]{2,1,0:T(8,128)S(1)}, f32[2,32,1024]{2,1,0:T(8,128)S(1)}, u32[]{:S(2)}, u32[]{:S(2)}) collective-permute-start(f32[2,32,1024]{2,1,0:T(8,128)S(1)} %get-tuple-element.35), channel_id=1, source_target_pairs={{1,0},{2,1},{3,2},{0,3},{5,4},{6,5},{7,6},{4,7},{9,8},{10,9},{11,1... | collective-permute-start | bytes 786440 | tf_op jit(solution)/shard_map/ppermute | solution.py:26
  245.2 36.4 %collective-permute-start.18 = (f32[1,32,2048]{2,1,0:T(8,128)S(1)}, f32[1,32,2048]{2,1,0:T(8,128)S(1)}, u32[]{:S(2)}, u32[]{:S(2)}) collective-permute-start(f32[1,32,2048]{2,1,0:T(8,128)S(1)} %get-tuple-element.32), channel_id=1, source_target_pairs={{0,4},{4,8},{8,12},{12,16},{16,20},{20,24},{24,28},{1,5},{5,9},{9,... | collective-permute-start | bytes 786440 | tf_op jit(solution)/shard_map/ppermute | solution.py:24
  246.6 35.1 %collective-permute-start.19 = (f32[1,32,2048]{2,1,0:T(8,128)S(1)}, f32[1,32,2048]{2,1,0:T(8,128)}, u32[]{:S(2)}, u32[]{:S(2)}) collective-permute-start(f32[1,32,2048]{2,1,0:T(8,128)S(1)} %get-tuple-element.33), channel_id=1, source_target_pairs={{4,0},{8,4},{12,8},{16,12},{20,16},{24,20},{28,24},{5,1},{9,5},{13... | collective-permute-start | bytes 786440 | tf_op jit(solution)/shard_map/ppermute | solution.py:26
  282.9 11.1 %collective-permute-start.20 = (f32[2,32,1024]{2,1,0:T(8,128)S(1)}, f32[2,32,1024]{2,1,0:T(8,128)S(1)}, u32[]{:S(2)}, u32[]{:S(2)}) collective-permute-start(f32[2,32,1024]{2,1,0:T(8,128)S(1)} %get-tuple-element.30), channel_id=1, source_target_pairs={{0,1},{1,2},{2,3},{3,0},{4,5},{5,6},{6,7},{7,4},{8,9},{9,10},{10,1... | collective-permute-start | bytes 786440 | tf_op jit(solution)/shard_map/ppermute | solution.py:24
  283.0 13.8 %collective-permute-start.21 = (f32[2,32,1024]{2,1,0:T(8,128)S(1)}, f32[2,32,1024]{2,1,0:T(8,128)S(1)}, u32[]{:S(2)}, u32[]{:S(2)}) collective-permute-start(f32[2,32,1024]{2,1,0:T(8,128)S(1)} %get-tuple-element.31), channel_id=1, source_target_pairs={{1,0},{2,1},{3,2},{0,3},{5,4},{6,5},{7,6},{4,7},{9,8},{10,9},{11,1... | collective-permute-start | bytes 786440 | tf_op jit(solution)/shard_map/ppermute | solution.py:26
  286.9 36.4 %collective-permute-start.22 = (f32[1,32,2048]{2,1,0:T(8,128)S(1)}, f32[1,32,2048]{2,1,0:T(8,128)S(1)}, u32[]{:S(2)}, u32[]{:S(2)}) collective-permute-start(f32[1,32,2048]{2,1,0:T(8,128)S(1)} %get-tuple-element.28), channel_id=1, source_target_pairs={{0,4},{4,8},{8,12},{12,16},{16,20},{20,24},{24,28},{1,5},{5,9},{9,... | collective-permute-start | bytes 786440 | tf_op jit(solution)/shard_map/ppermute | solution.py:24
  288.2 35.1 %collective-permute-start.23 = (f32[1,32,2048]{2,1,0:T(8,128)S(1)}, f32[1,32,2048]{2,1,0:T(8,128)S(1)}, u32[]{:S(2)}, u32[]{:S(2)}) collective-permute-start(f32[1,32,2048]{2,1,0:T(8,128)S(1)} %get-tuple-element.29), channel_id=1, source_target_pairs={{4,0},{8,4},{12,8},{16,12},{20,16},{24,20},{28,24},{5,1},{9,5},{13... | collective-permute-start | bytes 786440 | tf_op jit(solution)/shard_map/ppermute | solution.py:26
  372.5 12.6 %collective-permute-start.25 = (f32[2,32,1024]{2,1,0:T(8,128)S(1)}, f32[2,32,1024]{2,1,0:T(8,128)S(1)}, u32[]{:S(2)}, u32[]{:S(2)}) collective-permute-start(f32[2,32,1024]{2,1,0:T(8,128)S(1)} %get-tuple-element.27), channel_id=1, source_target_pairs={{1,0},{2,1},{3,2},{0,3},{5,4},{6,5},{7,6},{4,7},{9,8},{10,9},{11,1... | collective-permute-start | bytes 786440 | tf_op jit(solution)/shard_map/ppermute | solution.py:26
  375.9 33.6 %collective-permute-start.26 = (f32[1,32,2048]{2,1,0:T(8,128)}, f32[1,32,2048]{2,1,0:T(8,128)S(1)}, u32[]{:S(2)}, u32[]{:S(2)}) collective-permute-start(f32[1,32,2048]{2,1,0:T(8,128)} %get-tuple-element.24), channel_id=1, source_target_pairs={{0,4},{4,8},{8,12},{12,16},{16,20},{20,24},{24,28},{1,5},{5,9},{9,... | collective-permute-start | bytes 786440 | tf_op jit(solution)/shard_map/ppermute | solution.py:24
  377.2 32.3 %collective-permute-start.27 = (f32[1,32,2048]{2,1,0:T(8,128)}, f32[1,32,2048]{2,1,0:T(8,128)}, u32[]{:S(2)}, u32[]{:S(2)}) collective-permute-start(f32[1,32,2048]{2,1,0:T(8,128)} %get-tuple-element.25), channel_id=1, source_target_pairs={{4,0},{8,4},{12,8},{16,12},{20,16},{24,20},{28,24},{5,1},{9,5},{13... | collective-permute-start | bytes 786440 | tf_op jit(solution)/shard_map/ppermute | solution.py:26
  (7 other events, 155.0 us)
